TPU v7x, 256 devices: a whole 4x4x8 slice. The times are simulated.
256 devices in a mesh: pop: 32 (over x_lo, z, core), tp: 8 (over x_hi, y).
Axes of the slice: x: 4 (x_hi: 2, x_lo: 2; x = x_hi * 2 + x_lo), y: 4, z: 8, core: 2. Of those that a mesh axis runs over, the one named last changes fastest.
Arguments:
- hidden: bfloat16 [2048, 5120], P('pop', 'tp'), may hold values from -24 to 24
- norm_gain: float32 [5120], P('tp'), may hold values from 0.25 to 1.75
- right_factors: bfloat16 [5120, 128], P('tp'), may hold values from -0.078125 to 0.078125
- left_factors: bfloat16 [77824, 128], P(('pop', 'tp')), may hold values from -4 to 4
- targets: int32 [2048], replicated, may hold values from 0 to 77823
- master: float32 [77824, 5120], P(('pop', 'tp')), may hold values from -0.2934839 to 0.2934839
Outputs:
- member_loglik: float32 [64], replicated
- new_master: float32 [77824, 5120], P(('pop', 'tp'))
All inputs are finite; a program needn't handle non-finite values.
Results may differ from a plain program's by a relative error of at most 0.0026.
The roundings to bfloat16 on the way count: a program that leaves them out, or rounds other values in their place, can miss the bound.
Values may be sent and summed in bfloat16 or wider, within the bound.
A program may use at most 128 MiB of HBM per device.

v0:
```python
import jax
import jax.numpy as jnp
from jax import lax
from jax.sharding import PartitionSpec as P

D = 5120
RANK = 4
SEQ = 32
NORM_EPS = 1e-06
SIGMA_NOISE = 0.25
LEARN_RATE = 0.5


def contract(left, right):
    return lax.dot_general(
        left, right, (((1,), (1,)), ((), ())), preferred_element_type=jnp.float32
    )


def body(hidden, norm_gain, right_factors, left_factors, targets, master):
    tok_rows = hidden.shape[0]
    half_rows = tok_rows // 2
    fact_cols = right_factors.shape[1]
    voc_rows = master.shape[0]
    pop_index = lax.axis_index("pop")
    values = hidden.astype(jnp.float32)
    squares = lax.psum(jnp.sum(values * values, axis=1), "tp")
    row_scale = lax.rsqrt(squares / D + NORM_EPS)
    normed = (values * row_scale[:, None] * norm_gain[None, :]).astype(jnp.bfloat16)
    pair_cols = lax.dynamic_slice_in_dim(right_factors, pop_index * RANK, RANK, 1)
    partial_proj = jnp.dot(normed, pair_cols, preferred_element_type=jnp.float32)
    projection = lax.psum(partial_proj, "tp")
    member_sign = jnp.where(jnp.arange(tok_rows) < half_rows, SIGMA_NOISE, -SIGMA_NOISE).astype(
        jnp.float32
    )
    scaled = projection * member_sign[:, None]
    own_block = (lax.iota(jnp.int32, fact_cols) // RANK == pop_index).astype(jnp.float32)
    lowrank = (jnp.tile(scaled, (1, fact_cols // RANK)) * own_block[None, :]).astype(jnp.bfloat16)
    head = master.astype(jnp.bfloat16)
    full_rows, full_right = (
        lax.all_gather(normed, "tp", axis=1, tiled=True),
        lax.all_gather(right_factors, "tp", axis=0, tiled=True),
    )
    joined_rows = jnp.concatenate([full_rows, lowrank], axis=1)
    piece = lax.all_gather(joined_rows, "pop", axis=0, tiled=True)
    logits = contract(piece[:, :D], head) + contract(piece[:, D:], left_factors)
    offset = (pop_index * lax.axis_size("tp") + lax.axis_index("tp")) * voc_rows
    row_max = jnp.max(logits, axis=1)
    column_ids = lax.iota(jnp.int32, voc_rows)
    target_logit = jnp.sum(
        jnp.where(offset + column_ids[None, :] == targets[:, None], logits, 0.0), axis=1
    )
    all_max = lax.pmax(row_max, ("pop", "tp"))
    row_sum = jnp.sum(jnp.exp(logits - all_max[:, None]), axis=1)
    all_sum, all_target = lax.psum((row_sum, target_logit), ("pop", "tp"))
    logprob = all_target - all_max - jnp.log(all_sum)
    member_loglik = jnp.mean(logprob.reshape(-1, SEQ), axis=1)
    fitness = member_loglik[0::2] - member_loglik[1::2]
    weight_cols = jnp.repeat(fitness, RANK)
    scaled_left = (left_factors.astype(jnp.float32) * weight_cols[None, :]).astype(jnp.bfloat16)
    update = contract(scaled_left, full_right)
    new_master = master + LEARN_RATE * update
    return (member_loglik, new_master)


def solution(mesh):
    in_specs = (
        P("pop", "tp"),
        P("tp"),
        P("tp", None),
        P(("pop", "tp"), None),
        P(),
        P(("pop", "tp"), None),
    )
    out_specs = (P(), P(("pop", "tp"), None))
    return jax.shard_map(body, mesh=mesh, in_specs=in_specs, out_specs=out_specs, check_vma=False)
```

profile of v0, /device:TPU:1, one launch (start us, length us, event | category | flops | bytes accessed | tf_op | source)
XLA Modules:
  0.0 395.4 jit_solution(13763955117740881840)
XLA Ops:
  7.2 0.0 copy-start
  7.2 0.0 all-gather.3.cloned.1.call-start
  7.3 1.0 fusion.11
  8.3 21.5 %psum.28 = f32[64]{0:T(128)S(1)} all-reduce(f32[64]{0:T(128)S(1)} %fusion.11), channel_id=1, replica_groups=mesh['pop'=32,'tp'=8] {'tp'}, use_global_device_ids=true, to_apply=%region_1.0 | all-reduce | flops 64 | bytes 512 | tf_op jit(solution)/shard_map/psum | solution.py:27
  29.8 1.0 fusion.13
  30.8 29.9 %all_gather.9 = bf16[64,5120]{1,0:T(8,128)(2,1)S(1)} all-gather(bf16[64,640]{1,0:T(8,128)(2,1)S(1)} %fusion.13), channel_id=1, replica_groups=mesh['pop'=32,'tp'=8] {'tp'}, dimensions={1}, use_global_device_ids=true | all-gather | bytes 737280 | tf_op jit(solution)/shard_map/all_gather | solution.py:41
  60.7 1.2 fusion.14
  61.8 15.7 %psum.29 = f32[64,4]{0,1:T(4,128)S(1)} all-reduce(f32[64,4]{0,1:T(4,128)S(1)} %fusion.14), channel_id=1, replica_groups=mesh['pop'=32,'tp'=8] {'tp'}, use_global_device_ids=true, to_apply=%region_2.0 | all-reduce | flops 256 | bytes 2048 | tf_op jit(solution)/shard_map/psum | solution.py:32
  77.6 0.1 multiply_convert_fusion.2
  77.7 0.1 copy.9
  77.8 0.9 pad_maximum_fusion
  78.7 0.0 all-gather.3.cloned.1.call-update
  78.7 0.0 all-gather.5.cloned.1.call-start
  78.7 0.7 all-gather.5.cloned.1.call-update
  79.5 135.6 %all-gather.3.cloned.1.call-done = bf16[2048,5248]{1,0:T(8,128)(2,1)} async-done(((bf16[64,5248]{1,0:T(8,128)(2,1)}), bf16[2048,5248]{1,0:T(8,128)(2,1)}) %all-gather.3.cloned.1.call-update) | async-done | bytes 21495824 | tf_op jit(solution)/shard_map/all_gather | solution.py:45
  215.0 0.0 copy-done
  215.0 1.5 fusion.9
  216.6 0.0 copy-start.1
  216.6 12.6 %fusion.18 = (f32[2048]{0:T(1024)S(1)}, f32[2048,304]{0,1:T(8,128)S(1)}) fusion(f32[2048,304]{0,1:T(8,128)S(1)} %fusion.9, f32[304,5120]{1,0:T(8,128)} %param.11, bf16[2048,5248]{1,0:T(8,128)(2,1)} %all-gather.3.cloned.1.call-done), kind=kOutput, calls=%fused_computation.33 | convolution fusion | flops 6378141696 | bytes 32186368 | tf_op jit(solution)/shard_map/dot_general | solution.py:15
  229.2 78.5 %pmax.7 = f32[2048]{0:T(1024)S(1)} all-reduce(f32[2048]{0:T(1024)S(1)} %get-tuple-element.6), channel_id=1, replica_groups=mesh['pop'=32,'tp'=8] {'pop','tp'}, use_global_device_ids=true, to_apply=%region_6.7 | all-reduce | flops 2048 | bytes 16384 | tf_op jit(solution)/shard_map/pmax | solution.py:53
  307.8 0.0 copy-done.1
  307.8 0.6 select_reduce_fusion
  308.4 72.7 %all-reduce = (f32[2048]{0:T(1024)S(1)}, f32[2048]{0:T(1024)S(1)}) all-reduce(f32[2048]{0:T(1024)S(1)} %get-tuple-element.3, f32[2048]{0:T(1024)S(1)} %get-tuple-element.2), channel_id=1, replica_groups=mesh['pop'=32,'tp'=8] {'pop','tp'}, use_global_device_ids=true, to_apply=%region_8.9 | all-reduce | flops 4096 | bytes 32768 | tf_op jit(solution)/shard_map/psum | solution.py:55
  381.1 0.1 reshape.41
  381.1 0.1 reduce_sum.39
  381.3 0.0 copy-start.2
  381.3 0.1 slice.14
  381.4 0.1 slice.15
  381.5 0.1 broadcast_in_dim.25
  381.6 0.1 mul.72
  381.7 0.0 all-gather.5.cloned.1.call-done
  381.7 6.8 %fusion.2 = f32[304,5120]{1,0:T(8,128)} fusion(f32[304,5120]{1,0:T(8,128)} %param.11, bf16[5120,128]{1,0:T(8,128)(2,1)} %all-gather.5.cloned.1.call-done, bf16[304,128]{1,0:T(8,128)(2,1)S(1)} %copy-done, f32[128]{0:T(128)S(1)} %mul.72), kind=kOutput, calls=%fused_computation.3 | convolution fusion | flops 401688576 | bytes 13840896 | tf_op jit(solution)/shard_map/dot_general | solution.py:15
  388.6 0.0 copy-done.2
  (9 shorter events, 0.1 us)
Async XLA Ops:
  7.2 207.9 %copy-start = (bf16[304,128]{1,0:T(8,128)(2,1)S(1)}, bf16[304,128]{1,0:T(8,128)(2,1)}, u32[]{:S(2)}) copy-start(bf16[304,128]{1,0:T(8,128)(2,1)} %param.9) | copy-start | bytes 233476
  7.2 207.9 %all-gather.3.cloned.1.call-start = ((), (), s32[]{:S(2)}) async-start(), calls=%async_computation | async-start | bytes 22167552 | tf_op jit(solution)/shard_map/all_gather | solution.py:45
  78.7 303.1 %all-gather.5.cloned.1.call-start = ((), (), s32[]{:S(2)}) async-start(), calls=%async_computation.1 | async-start | bytes 1474560 | tf_op jit(solution)/shard_map/all_gather | solution.py:42
  216.6 91.2 %copy-start.1 = (s32[2048]{0:T(1024)S(1)}, s32[2048]{0:T(1024)}, u32[]{:S(2)}) copy-start(s32[2048]{0:T(1024)} %param.10) | copy-start | bytes 24580
  381.3 7.3 %copy-start.2 = (f32[64]{0:T(128)}, f32[64]{0:T(128)S(1)}, u32[]{:S(2)}) copy-start(f32[64]{0:T(128)S(1)} %broadcast_multiply_fusion.1) | copy-start | bytes 772
Sparse Core Ops, SparseCore 0:
  78.8 136.1 all-gather.2
  217.6 52.0 all-gather.4
where the time goes:
time: 396 us; the launch traced here: 395 us
  blocking collectives  218 us (55%)
  waiting for transfers between devices  136 us (34%)
  matrix products  22.2 us (6%)
  between operations  14.2 us (4%)
    all_gather x1, waiting for transfers between devices, body(): piece = lax.all_gather(joined_rows, 'pop', axis=0, tiled=True)  136 us
    pmax x1, blocking collectives, body(): all_max = lax.pmax(row_max, ('pop', 'tp'))  78.5 us
    psum x1, blocking collectives, body(): all_sum, all_target = lax.psum((row_sum, target_logit), ('pop', 'tp'))  72.7 us
    all_gather x1, blocking collectives, body(): lax.all_gather(normed, 'tp', axis=1, tiled=True)  29.9 us
    psum x1, blocking collectives, body(): squares = lax.psum(jnp.sum(values * values, axis=1), 'tp')  21.5 us
    dot_general x3, matrix products, contract(): lax.dot_general(left, right, (((1,), (1,)), ((), ())), preferred_element_...  21 us
    psum x1, blocking collectives, body(): projection = lax.psum(partial_proj, 'tp')  15.7 us
  transfers between devices with their start and end apart: 2, of which 1 were waited for; matrix products, arithmetic and copies ran while one was open for 4% of the time, Pallas kernels for 0%

commit v1 on v0

--- a/solution.py
+++ b/solution.py
@@ -52,7 +52,7 @@
     )
     all_max = lax.pmax(row_max, ("pop", "tp"))
     row_sum = jnp.sum(jnp.exp(logits - all_max[:, None]), axis=1)
-    all_sum, all_target = lax.psum((row_sum, target_logit), ("pop", "tp"))
+    all_sum, all_target = lax.psum(lax.psum((row_sum, target_logit), "tp"), "pop")
     logprob = all_target - all_max - jnp.log(all_sum)
     member_loglik = jnp.mean(logprob.reshape(-1, SEQ), axis=1)
     fitness = member_loglik[0::2] - member_loglik[1::2]

time: 396 us -> 465 us (1.17)
  blocking collectives: 218 us -> 284 us
    psum x1 -> x2, blocking collectives: 72.7 us -> 138 us  [the longest x1 108 us: body(): lax.psum(lax.psum((row_sum, target_logit), 'tp'), 'pop')]
  transfers between devices with their start and end apart: 2 -> 2, of which waited for: 1 -> 1; matrix products, arithmetic and copies ran while one was open for 4% -> 3% of each run, Pallas kernels for 0% -> 0%
where the time goes in v1:
time: 465 us; the launch traced here: 461 us
  blocking collectives  284 us (61%)
  waiting for transfers between devices  136 us (29%)
  matrix products  22.2 us (5%)
  between operations  14.2 us (3%)
    all_gather x1, waiting for transfers between devices, body(): piece = lax.all_gather(joined_rows, 'pop', axis=0, tiled=True)  136 us
    psum x1, blocking collectives, body(): lax.psum(lax.psum((row_sum, target_logit), 'tp'), 'pop')  108 us
    pmax x1, blocking collectives, body(): all_max = lax.pmax(row_max, ('pop', 'tp'))  78.6 us
    psum x1, blocking collectives, body(): lax.psum((row_sum, target_logit), 'tp')  30.5 us
    all_gather x1, blocking collectives, body(): lax.all_gather(normed, 'tp', axis=1, tiled=True)  29.9 us
    psum x1, blocking collectives, body(): squares = lax.psum(jnp.sum(values * values, axis=1), 'tp')  21.5 us
    dot_general x3, matrix products, contract(): lax.dot_general(left, right, (((1,), (1,)), ((), ())), preferred_element_...  21 us
    psum x1, blocking collectives, body(): projection = lax.psum(partial_proj, 'tp')  15.7 us
  transfers between devices with their start and end apart: 2, of which 1 were waited for; matrix products, arithmetic and copies ran while one was open for 3% of the time, Pallas kernels for 0%

profile of v1, /device:TPU:1, one launch (start us, length us, event | category | flops | bytes accessed | tf_op | source)
XLA Modules:
  0.0 460.9 jit_solution(10950857298111984443)
XLA Ops:
  7.2 0.0 copy-start
  7.2 0.0 all-gather.3.cloned.1.call-start
  7.3 1.0 fusion.11
  8.3 21.5 %psum.42 = f32[64]{0:T(128)S(1)} all-reduce(f32[64]{0:T(128)S(1)} %fusion.11), channel_id=1, replica_groups=mesh['pop'=32,'tp'=8] {'tp'}, use_global_device_ids=true, to_apply=%region_1.0 | all-reduce | flops 64 | bytes 512 | tf_op jit(solution)/shard_map/psum | solution.py:27
  29.8 1.0 fusion.13
  30.8 29.9 %all_gather.9 = bf16[64,5120]{1,0:T(8,128)(2,1)S(1)} all-gather(bf16[64,640]{1,0:T(8,128)(2,1)S(1)} %fusion.13), channel_id=1, replica_groups=mesh['pop'=32,'tp'=8] {'tp'}, dimensions={1}, use_global_device_ids=true | all-gather | bytes 737280 | tf_op jit(solution)/shard_map/all_gather | solution.py:41
  60.7 1.2 fusion.14
  61.8 15.7 %psum.43 = f32[64,4]{0,1:T(4,128)S(1)} all-reduce(f32[64,4]{0,1:T(4,128)S(1)} %fusion.14), channel_id=1, replica_groups=mesh['pop'=32,'tp'=8] {'tp'}, use_global_device_ids=true, to_apply=%region_2.0 | all-reduce | flops 256 | bytes 2048 | tf_op jit(solution)/shard_map/psum | solution.py:32
  77.6 0.1 multiply_convert_fusion.2
  77.7 0.1 copy.9
  77.8 0.9 pad_maximum_fusion
  78.7 0.0 all-gather.3.cloned.1.call-update
  78.7 0.0 all-gather.5.cloned.1.call-start
  78.7 0.7 all-gather.5.cloned.1.call-update
  79.5 135.6 %all-gather.3.cloned.1.call-done = bf16[2048,5248]{1,0:T(8,128)(2,1)} async-done(((bf16[64,5248]{1,0:T(8,128)(2,1)}), bf16[2048,5248]{1,0:T(8,128)(2,1)}) %all-gather.3.cloned.1.call-update) | async-done | bytes 21495824 | tf_op jit(solution)/shard_map/all_gather | solution.py:45
  215.0 0.0 copy-done
  215.0 1.5 fusion.9
  216.6 0.0 copy-start.1
  216.6 12.6 %fusion.18 = (f32[2048]{0:T(1024)S(1)}, f32[2048,304]{0,1:T(8,128)S(1)}) fusion(f32[2048,304]{0,1:T(8,128)S(1)} %fusion.9, f32[304,5120]{1,0:T(8,128)} %param.11, bf16[2048,5248]{1,0:T(8,128)(2,1)} %all-gather.3.cloned.1.call-done), kind=kOutput, calls=%fused_computation.33 | convolution fusion | flops 6378141696 | bytes 32186368 | tf_op jit(solution)/shard_map/dot_general | solution.py:15
  229.2 78.6 %pmax.7 = f32[2048]{0:T(1024)S(1)} all-reduce(f32[2048]{0:T(1024)S(1)} %get-tuple-element.8), channel_id=1, replica_groups=mesh['pop'=32,'tp'=8] {'pop','tp'}, use_global_device_ids=true, to_apply=%region_7.8 | all-reduce | flops 2048 | bytes 16384 | tf_op jit(solution)/shard_map/pmax | solution.py:53
  307.8 0.0 copy-done.1
  307.8 0.6 select_reduce_fusion
  308.4 30.5 %all-reduce.1 = (f32[2048]{0:T(1024)S(1)}, f32[2048]{0:T(1024)S(1)}) all-reduce(f32[2048]{0:T(1024)S(1)} %get-tuple-element.3, f32[2048]{0:T(1024)S(1)} %get-tuple-element.2), channel_id=1, replica_groups=mesh['pop'=32,'tp'=8] {'tp'}, use_global_device_ids=true, to_apply=%region_9.10 | all-reduce | flops 4096 | bytes 32768 | tf_op jit(solution)/shard_map/psum | solution.py:55
  338.9 107.7 %all-reduce = (f32[2048]{0:T(1024)S(1)}, f32[2048]{0:T(1024)S(1)}) all-reduce(f32[2048]{0:T(1024)S(1)} %get-tuple-element.6, f32[2048]{0:T(1024)S(1)} %get-tuple-element.7), channel_id=1, replica_groups=mesh['pop'=32,'tp'=8] {'pop'}, use_global_device_ids=true, to_apply=%region_10.11 | all-reduce | flops 4096 | bytes 32768 | tf_op jit(solution)/shard_map/psum | solution.py:55
  446.6 0.1 reshape.41
  446.6 0.1 reduce_sum.39
  446.8 0.0 copy-start.2
  446.8 0.1 slice.14
  446.9 0.1 slice.15
  447.0 0.1 broadcast_in_dim.25
  447.1 0.1 mul.72
  447.2 0.0 all-gather.5.cloned.1.call-done
  447.3 6.8 %fusion.2 = f32[304,5120]{1,0:T(8,128)} fusion(f32[304,5120]{1,0:T(8,128)} %param.11, bf16[5120,128]{1,0:T(8,128)(2,1)} %all-gather.5.cloned.1.call-done, bf16[304,128]{1,0:T(8,128)(2,1)S(1)} %copy-done, f32[128]{0:T(128)S(1)} %mul.72), kind=kOutput, calls=%fused_computation.3 | convolution fusion | flops 401688576 | bytes 13840896 | tf_op jit(solution)/shard_map/dot_general | solution.py:15
  454.1 0.0 copy-done.2
  (9 shorter events, 0.1 us)
Async XLA Ops:
  7.2 207.9 %copy-start = (bf16[304,128]{1,0:T(8,128)(2,1)S(1)}, bf16[304,128]{1,0:T(8,128)(2,1)}, u32[]{:S(2)}) copy-start(bf16[304,128]{1,0:T(8,128)(2,1)} %param.9) | copy-start | bytes 233476
  7.2 207.9 %all-gather.3.cloned.1.call-start = ((), (), s32[]{:S(2)}) async-start(), calls=%async_computation | async-start | bytes 22167552 | tf_op jit(solution)/shard_map/all_gather | solution.py:45
  78.7 368.6 %all-gather.5.cloned.1.call-start = ((), (), s32[]{:S(2)}) async-start(), calls=%async_computation.1 | async-start | bytes 1474560 | tf_op jit(solution)/shard_map/all_gather | solution.py:42
  216.6 91.2 %copy-start.1 = (s32[2048]{0:T(1024)S(1)}, s32[2048]{0:T(1024)}, u32[]{:S(2)}) copy-start(s32[2048]{0:T(1024)} %param.10) | copy-start | bytes 24580
  446.8 7.3 %copy-start.2 = (f32[64]{0:T(128)}, f32[64]{0:T(128)S(1)}, u32[]{:S(2)}) copy-start(f32[64]{0:T(128)S(1)} %broadcast_multiply_fusion.1) | copy-start | bytes 772
Sparse Core Ops, SparseCore 0:
  78.8 136.1 all-gather.2
  217.6 52.0 all-gather.4
